TPU v7x, 128 devices: a whole 4x4x4 slice. The times are simulated.
128 devices in a mesh: dp: 32 (over x, y_lo, z), gz: 4 (over y_hi, core).
Axes of the slice: x: 4, y: 4 (y_hi: 2, y_lo: 2; y = y_hi * 2 + y_lo), z: 4, core: 2. Of those that a mesh axis runs over, the one named last changes fastest.
Arguments:
- field: bfloat16 [32, 16, 96, 9216], P('dp', None, 'gz'), may hold values from -6 to 6
- cotangent: bfloat16 [32, 16, 96, 9216], P('dp', None, 'gz'), may hold values from -36 to 36, as said below
- spec_weight: float32 [16, 16, 16, 256], P('gz'), may hold values from -1.5 to 1.5
- point_weight: bfloat16 [16, 16], replicated, may hold values from -1.5 to 1.5
- bias: float32 [16], replicated, may hold values from -3 to 3
Outputs:
- field_grad: bfloat16 [32, 16, 96, 9216], P('dp', None, 'gz')
- spectral_grad: float32 [16, 16, 16, 256], P('gz')
- point_grad: float32 [16, 16], replicated
- bias_grad: float32 [16], replicated
Inputs may be any that keep to these rules, and one draw needn't show every extreme that they name: `cotangent`: the gradient of the loss with respect to the layer's output.
All inputs are finite; a program needn't handle non-finite values.
Results may differ from a plain program's by a relative error of at most 0.007.
Values sent between devices are 32-bit elements; how exact they have to be, the bound alone decides.
No kernel may reach another device: no remote copies, remote signals or barrier semaphores. Data moves between devices by JAX's collectives and lax.ppermute only.
A program may use at most 192 MiB of HBM per device.

v0:
```python
import math
import jax
import jax.numpy as jnp
from jax import lax
from jax.sharding import PartitionSpec as P

N = 96
M = 16
root_half = 0.7071067811865476
density_norm = 0.3989422804014327


def basis_table(count_modes, length):
    mode_index = jnp.arange(count_modes, dtype=jnp.int32)
    half_count = count_modes // 2
    frequency = jnp.where(mode_index < half_count, mode_index, mode_index - half_count + 1)
    position = jnp.arange(length, dtype=jnp.int32)
    turns = frequency[:, None] * position[None, :] % length
    angle = turns.astype(jnp.float32) * (2.0 * math.pi / length)
    return jnp.where((mode_index < half_count)[:, None], jnp.cos(angle), jnp.sin(angle))


def kron_table(basis):
    outer = basis[:, None, :, None] * basis[None, :, None, :]
    return outer.reshape(M * M, N * N)


def gelu_slope(values):
    cumulative = 0.5 * (1.0 + lax.erf(values * root_half))
    return cumulative + values * jnp.exp(-0.5 * values * values) * density_norm


def shards(field, cotangent, spec_weight, point_weight, bias):
    highest = lax.Precision.HIGHEST
    samples_dev, channels, slab_rows, plane_cells = field.shape
    scale_fwd = (2.0 / N) ** 1.5
    scale_inv = (2.0 / M) ** 1.5
    basis = basis_table(M, N)
    kron = kron_table(basis)
    row_basis = lax.dynamic_slice_in_dim(basis, lax.axis_index("gz") * slab_rows, slab_rows, 1)
    contract_cells = (((1,), (1,)), ((), ()))

    def to_modes(values):
        flattened = values.reshape(samples_dev * channels * slab_rows, plane_cells).astype(
            jnp.float32
        )
        return lax.dot_general(flattened, kron, contract_cells, precision=highest).reshape(
            samples_dev, channels, slab_rows, M * M
        )

    def add_inverse(piece):
        piece_rows = piece.shape[0]
        inner = jnp.dot(
            piece.reshape(piece_rows * samples_dev * channels, M * M), kron, precision=highest
        )
        inner = inner.reshape(piece_rows, samples_dev, channels, plane_cells)
        return jnp.einsum("ax,asoz->soxz", row_basis, inner, precision=highest)

    line_modes = to_modes(field)
    rows_part = row_basis
    coefficients = lax.psum_scatter(
        scale_fwd * jnp.einsum("ax,scxp->ascp", rows_part, line_modes, precision=highest),
        "gz",
        scatter_dimension=0,
        tiled=True,
    )
    mixed_modes = jnp.einsum("asip,aiop->asop", coefficients, spec_weight, precision=highest)
    spectral = scale_inv * add_inverse(lax.all_gather(mixed_modes, "gz", axis=0, tiled=True))
    pre_act = (
        spectral
        + jnp.einsum("sixz,io->soxz", field, point_weight, preferred_element_type=jnp.float32)
        + bias[None, :, None, None]
    )
    grad_pre = (cotangent.astype(jnp.float32) * gelu_slope(pre_act)).astype(jnp.bfloat16)
    grad_line = to_modes(grad_pre)
    rows_part = row_basis
    grad_modes = lax.psum_scatter(
        scale_inv * jnp.einsum("ax,soxp->asop", rows_part, grad_line, precision=highest),
        "gz",
        scatter_dimension=0,
        tiled=True,
    )
    back_modes = jnp.einsum("aiop,asop->asip", spec_weight, grad_modes, precision=highest)
    field_spec = scale_fwd * add_inverse(lax.all_gather(back_modes, "gz", axis=0, tiled=True))
    field_grad = (
        field_spec
        + jnp.einsum("soxz,io->sixz", grad_pre, point_weight, preferred_element_type=jnp.float32)
    ).astype(jnp.bfloat16)
    local_point = jnp.einsum("sixz,soxz->io", field, grad_pre, preferred_element_type=jnp.float32)
    local_bias = jnp.sum(grad_pre, axis=(0, 2, 3), dtype=jnp.float32)
    total_point, total_bias = lax.psum((local_point, local_bias), ("dp", "gz"))
    local_spec = jnp.einsum("asip,asop->aiop", coefficients, grad_modes, precision=highest)
    grad_spec = lax.psum(local_spec, "dp")
    all_samples = samples_dev * lax.axis_size("dp")
    cell_norm = math.sqrt(all_samples * N * N * N)
    return (
        field_grad,
        grad_spec / math.sqrt(all_samples * N),
        total_point / cell_norm,
        total_bias / cell_norm,
    )


def solution(mesh):
    return jax.shard_map(
        shards,
        mesh=mesh,
        in_specs=(
            P("dp", None, "gz", None),
            P("dp", None, "gz", None),
            P("gz", None, None, None),
            P(),
            P(),
        ),
        out_specs=(P("dp", None, "gz", None), P("gz", None, None, None), P(), P()),
        check_vma=False,
    )
```

profile of v0, /device:TPU:0, one launch (start us, length us, event | category | flops | bytes accessed | tf_op | source)
XLA Modules:
  0.0 559.2 jit_solution(4819427986787261615)
XLA Ops:
  7.4 6.2 %broadcast_multiply_fusion = f32[16,16,96,96]{3,2,1,0:T(8,128)} fusion(f32[16,96]{1,0:T(8,128)S(1)} %sine_select_fusion), kind=kLoop, calls=%fused_computation.12 | loop fusion | flops 2359296 | bytes 9443328 | tf_op jit(solution)/shard_map/mul | solution.py:24
  13.6 12.8 %mul.213 = f32[256,9216]{1,0:T(8,128)} reshape(f32[16,16,96,96]{3,2,1,0:T(8,128)} %broadcast_multiply_fusion) | data formatting | bytes 18874368 | tf_op jit(solution)/shard_map/mul | solution.py:24
  26.4 11.1 %convolution_bitcast_fusion = f32[384,256]{0,1:T(8,128)S(1)} fusion(f32[256,9216]{1,0:T(8,128)} %mul.213, bf16[384,9216]{1,0:T(8,128)(2,1)} %bitcast.98), kind=kOutput, calls=%fused_computation.20 | convolution fusion | flops 10871635968 | bytes 16908288 | tf_op jit(solution)/shard_map/dot_general | solution.py:47
  38.1 0.9 copy.32
  39.0 12.9 %reshape.211 = f32[256,9216,1]{1,0,2:T(8,128)} reshape(f32[16,16,96,96]{3,2,1,0:T(8,128)} %broadcast_multiply_fusion) | data formatting | bytes 18874368 | tf_op jit(solution)/shard_map/mul | solution.py:24
  51.9 11.7 %fusion.13 = f32[16,24,9216]{2,0,1:T(8,128)} fusion(bf16[16,24,9216]{2,1,0:T(8,128)(2,1)} %bitcast.99, bf16[16,16]{1,0:T(8,128)(2,1)S(1)} %copy-done), kind=kOutput, calls=%fused_computation.18 | convolution fusion | flops 113246208 | bytes 21234176 | tf_op jit(solution)/shard_map/sixz,io->soxz/dot_general | solution.py:71
  63.6 5.0 reduce-scatter.3.cloned.1.call-done
  68.6 1.1 multiply_reduce_fusion.1
  69.8 7.4 %all_gather.6 = f32[16,1,16,256]{3,2,1,0:T(8,128)S(1)} all-gather(f32[4,1,16,256]{3,2,1,0:T(8,128)S(1)} %bitcast.109), channel_id=1, replica_groups=mesh['dp'=32,'gz'=4] {'gz'}, dimensions={0}, use_global_device_ids=true | all-gather | bytes 327680 | tf_op jit(solution)/shard_map/all_gather | solution.py:68
  77.2 12.2 %fusion.24 = f32[16,16,9216]{2,0,1:T(8,128)S(1)} fusion(f32[256,9216,1]{1,0,2:T(8,128)} %reshape.211, f32[16,1,16,256]{3,2,1,0:T(8,128)S(1)} %all_gather.6), kind=kOutput, calls=%fused_computation.32 | convolution fusion | flops 7247757312 | bytes 19136512 | tf_op jit(solution)/shard_map/dot_general | solution.py:53
  89.4 25.9 %convert_reduce_fusion = (f32[16]{0:T(128)S(1)}, bf16[1,16,24,9216]{3,2,1,0:T(8,128)(2,1)}) fusion(f32[16]{0:T(128)S(1)} %copy-done.3, f32[16,24,9216]{2,0,1:T(8,128)} %fusion.13, f32[16,16,9216]{2,0,1:T(8,128)S(1)} %fusion.24, f32[16,96]{1,0:T(8,128)S(1)} %sine_select_fusion, s32[]{:T(128)S(6)} %select_n.65, bf16[1,16,24,9216]{3,2,1,0:T(8,128)(2,1)S(1)} %bitcast.112), kind=kOutput, calls=%fused_computation.11 | convolution fusion | flops 736100352 | bytes 37755012 | tf_op jit(solution)/shard_map/ax,asoz->soxz/dot_general | solution.py:57
  115.4 13.4 %fusion.47 = f32[16,24,256]{2,1,0:T(8,128)S(1)} fusion(f32[256,9216,1]{1,0,2:T(8,128)S(1)} %bitcast.97, bf16[1,16,24,9216]{3,2,1,0:T(8,128)(2,1)} %get-tuple-element.21), kind=kOutput, calls=%fused_computation.62 | convolution fusion | flops 10871635968 | bytes 16908288 | tf_op jit(solution)/shard_map/dot_general | solution.py:47
  128.9 17.8 %fusion.17 = f32[16,16]{0,1:T(8,128)S(1)} fusion(bf16[16,24,9216]{2,1,0:T(8,128)(2,1)S(1)} %bitcast.102, bf16[16,24,9216]{2,1,0:T(8,128)(2,1)} %bitcast.103), kind=kOutput, calls=%fused_computation.25 | convolution fusion | flops 113246208 | bytes 14156800 | tf_op jit(solution)/shard_map/sixz,soxz->io/dot_general | solution.py:89
  146.7 65.4 %all-reduce = (f32[16,16]{0,1:T(8,128)S(1)}, f32[16]{0:T(128)S(1)}) all-reduce(f32[16,16]{0,1:T(8,128)S(1)} %fusion.17, f32[16]{0:T(128)S(1)} %get-tuple-element.20), channel_id=1, replica_groups=mesh['dp'=32,'gz'=4] {'dp','gz'}, use_global_device_ids=true, to_apply=%region_3.4 | all-reduce | flops 272 | bytes 2176 | tf_op jit(solution)/shard_map/psum | solution.py:91
  212.2 0.7 copy.43
  213.8 0.9 copy.37
  214.7 16.0 %fusion.10 = f32[24,9216,16]{1,2,0:T(8,128)} fusion(bf16[16,24,9216]{2,1,0:T(8,128)(2,1)} %bitcast.104, bf16[16,16]{1,0:T(8,128)(2,1)S(1)} %copy-done), kind=kOutput, calls=%fused_computation.15 | convolution fusion | flops 113246208 | bytes 21234176 | tf_op jit(solution)/shard_map/soxz,io->sixz/dot_general | solution.py:87
  230.7 8.1 %reduce-scatter.5.cloned.1.call-done = f32[4,1,16,256]{3,2,1,0:T(8,128)} async-done(((f32[16,1,16,256]{3,2,1,0:T(8,128)}), f32[4,1,16,256]{3,2,1,0:T(8,128)}) %reduce-scatter.5.cloned.1.call-update) | async-done | bytes 65552 | tf_op jit(solution)/shard_map/reduce_scatter | solution.py:77
  238.8 2.1 multiply_bitcast_fusion
  240.9 7.3 %all_gather.7 = f32[16,1,16,256]{3,2,1,0:T(8,128)S(1)} all-gather(f32[4,1,16,256]{3,2,1,0:T(8,128)S(1)} %bitcast.108), channel_id=1, replica_groups=mesh['dp'=32,'gz'=4] {'gz'}, dimensions={0}, use_global_device_ids=true | all-gather | bytes 327680 | tf_op jit(solution)/shard_map/all_gather | solution.py:84
  248.2 12.2 %fusion.22 = f32[16,16,9216]{2,0,1:T(8,128)S(1)} fusion(f32[256,9216,1]{1,0,2:T(8,128)} %reshape.211, f32[16,1,16,256]{3,2,1,0:T(8,128)S(1)} %all_gather.7), kind=kOutput, calls=%fused_computation.30 | convolution fusion | flops 7247757312 | bytes 19136512 | tf_op jit(solution)/shard_map/dot_general | solution.py:53
  260.4 25.8 %fusion.6 = bf16[1,16,24,9216]{3,2,1,0:T(8,128)(2,1)} fusion(f32[24,9216,16]{1,2,0:T(8,128)} %fusion.10, f32[16,16,9216]{2,0,1:T(8,128)S(1)} %fusion.22, f32[16,96]{1,0:T(8,128)S(1)} %sine_select_fusion, s32[]{:T(128)S(6)} %select_n.65), kind=kOutput, calls=%fused_computation.8 | convolution fusion | flops 690094080 | bytes 30676996 | tf_op jit(solution)/shard_map/ax,asoz->soxz/dot_general | solution.py:57
  286.2 263.8 %all-reduce.3.cloned.1.call-done = f32[4,16,16,256]{3,2,1,0:T(8,128)} async-done(((f32[4,16,16,256]{3,2,1,0:T(8,128)}), f32[4,16,16,256]{3,2,1,0:T(8,128)}) %all-reduce.3.cloned.1.call-update) | async-done | bytes 1048592 | tf_op jit(solution)/shard_map/psum | solution.py:93
  550.0 2.3 broadcast_multiply_fusion.1
  (39 shorter events, 1.9 us)
Async XLA Ops:
  7.2 44.8 %copy-start = (bf16[16,16]{1,0:T(8,128)(2,1)S(1)}, bf16[16,16]{1,0:T(8,128)(2,1)}, u32[]{:S(2)}) copy-start(bf16[16,16]{1,0:T(8,128)(2,1)} %param.8) | copy-start | bytes 1540
  7.2 61.4 %reduce-scatter.3.cloned.1.call-start = ((), (), s32[]{:S(2)}) async-start(), calls=%async_computation.2 | async-start | bytes 327680 | tf_op jit(solution)/shard_map/reduce_scatter | solution.py:61
  39.0 199.8 %reduce-scatter.5.cloned.1.call-start = ((), (), s32[]{:S(2)}) async-start(), calls=%async_computation.3 | async-start | bytes 327680 | tf_op jit(solution)/shard_map/reduce_scatter | solution.py:77
  51.9 16.7 %copy-start.1 = (f32[4,16,16,256]{3,2,1,0:T(8,128)S(1)}, f32[4,16,16,256]{3,2,1,0:T(8,128)}, u32[]{:S(2)}) copy-start(f32[4,16,16,256]{3,2,1,0:T(8,128)} %param.7) | copy-start | bytes 3145732
  68.6 20.8 %slice-start.5 = ((s8[7077888]{0:T(1024)(128)(4,1)}), s8[4194304]{0:T(1024)(128)(4,1)S(1)}, s32[]{:S(2)}) async-start(s8[7077888]{0:T(1024)(128)(4,1)} %bitcast.111), calls=%async_computation.10 | async-start | bytes 8388608
  77.2 12.2 %slice-start.6 = ((s8[7077888]{0:T(1024)(128)(4,1)}), s8[2883584]{0:T(1024)(128)(4,1)S(1)}, s32[]{:S(2)}) async-start(s8[7077888]{0:T(1024)(128)(4,1)} %bitcast.111), calls=%async_computation.11 | async-start | bytes 5767168
  77.2 12.2 %copy-start.3 = (f32[16]{0:T(128)S(1)}, f32[16]{0:T(128)}, u32[]{:S(2)}) copy-start(f32[16]{0:T(128)} %param.9) | copy-start | bytes 196
  77.2 38.2 %slice-start = ((s8[9437184]{0:T(1024)(128)(4,1)}), s8[4194304]{0:T(1024)(128)(4,1)S(1)}, s32[]{:S(2)}) async-start(s8[9437184]{0:T(1024)(128)(4,1)} %bitcast.96), calls=%async_computation.5 | async-start | bytes 8388608
  89.4 26.0 %slice-start.1 = ((s8[9437184]{0:T(1024)(128)(4,1)}), s8[4194304]{0:T(1024)(128)(4,1)S(1)}, s32[]{:S(2)}) async-start(s8[9437184]{0:T(1024)(128)(4,1)} %bitcast.96), calls=%async_computation.6 | async-start | bytes 8388608
  89.4 26.0 %slice-start.2 = ((s8[9437184]{0:T(1024)(128)(4,1)}), s8[1048576]{0:T(1024)(128)(4,1)S(1)}, s32[]{:S(2)}) async-start(s8[9437184]{0:T(1024)(128)(4,1)} %bitcast.96), calls=%async_computation.7 | async-start | bytes 2097152
  115.4 13.5 %slice-start.3 = ((s8[7077888]{0:T(1024)(128)(4,1)}), s8[4194304]{0:T(1024)(128)(4,1)S(1)}, s32[]{:S(2)}) async-start(s8[7077888]{0:T(1024)(128)(4,1)} %bitcast.100), calls=%async_computation.8 | async-start | bytes 8388608
  115.4 13.4 %slice-start.4 = ((s8[7077888]{0:T(1024)(128)(4,1)}), s8[2883584]{0:T(1024)(128)(4,1)S(1)}, s32[]{:S(2)}) async-start(s8[7077888]{0:T(1024)(128)(4,1)} %bitcast.100), calls=%async_computation.9 | async-start | bytes 5767168
  214.7 24.1 %copy-start.2 = (f32[4,1,16,256]{3,2,1,0:T(8,128)S(1)}, f32[4,1,16,256]{3,2,1,0:T(8,128)}, u32[]{:S(2)}) copy-start(f32[4,1,16,256]{3,2,1,0:T(8,128)} %reduce-scatter.3.cloned.1.call-done) | copy-start | bytes 196612
  214.7 335.3 %all-reduce.3.cloned.1.call-start = ((), (), s32[]{:S(2)}) async-start(), calls=%async_computation.4 | async-start | bytes 2097152 | tf_op jit(solution)/shard_map/psum | solution.py:93
Sparse Core Ops, SparseCore 0:
  39.1 29.4 reduce-scatter.2
  214.8 23.9 reduce-scatter.4
  241.8 308.1 all-reduce.2
where the time goes:
time: 568 us; the launch traced here: 559 us
  waiting for transfers between devices  277 us (49%)
  matrix products  147 us (26%)
  blocking collectives  80.2 us (14%)
  local copies, waits for them, and re-layouts  28.3 us (5%)
  between operations  14.3 us (3%)
  other arithmetic  12.4 us (2%)
    psum x1, waiting for transfers between devices, shards(): grad_spec = lax.psum(local_spec, 'dp')  264 us
    psum x1, blocking collectives, shards(): total_point, total_bias = lax.psum((local_point, local_bias), ('dp', 'gz'))  65.4 us
    dot_general x2, matrix products, add_inverse(): return jnp.einsum('ax,asoz->soxz', row_basis, inner, precision=highest)  51.8 us
    mul x2, local copies, waits for them, and re-layouts, kron_table(): outer = basis[:, None, :, None] * basis[None, :, None, :]  25.7 us
    dot_general x2, matrix products, to_modes(): lax.dot_general(flattened, kron, contract_cells, precision=highest)  24.5 us
    dot_general x2, matrix products, add_inverse(): jnp.dot(piece.reshape(piece_rows * samples_dev * channels, M * M), kron,...  24.4 us
    dot_general x1, matrix products, shards(): jnp.einsum('sixz,soxz->io', field, grad_pre, preferred_element_type=jnp.f...  17.8 us
    dot_general x1, matrix products, shards(): jnp.einsum('soxz,io->sixz', grad_pre, point_weight, preferred_element_typ...  16 us
  transfers between devices with their start and end apart: 3, of which 3 were waited for; matrix products, arithmetic and copies ran while one was open for 14% of the time, Pallas kernels for 0%

commit v1 on v0

--- a/solution.py
+++ b/solution.py
@@ -90,7 +90,7 @@
     local_bias = jnp.sum(grad_pre, axis=(0, 2, 3), dtype=jnp.float32)
     total_point, total_bias = lax.psum((local_point, local_bias), ("dp", "gz"))
     local_spec = jnp.einsum("asip,asop->aiop", coefficients, grad_modes, precision=highest)
-    grad_spec = lax.psum(local_spec, "dp")
+    grad_spec = jnp.sum(lax.all_gather(local_spec, "dp"), axis=0)
     all_samples = samples_dev * lax.axis_size("dp")
     cell_norm = math.sqrt(all_samples * N * N * N)
     return (

time: 568 us -> 660 us (1.16)
  blocking collectives: 80.2 us -> 412 us
  waiting for transfers between devices: 277 us -> 31.1 us
  other arithmetic: 12.4 us -> 23.4 us
    psum x1, blocking collectives: 65.4 us -> 387 us  [shards(): total_point, total_bias = lax.psum((local_point, local_bias), ('dp', 'gz'))]
    psum x1 -> x0, waiting for transfers between devices: 264 us -> none  [shards(): grad_spec = lax.psum(local_spec, 'dp')]
    reduce_scatter x1, waiting for transfers between devices: 8.07 us -> 26.1 us  [shards(): lax.psum_scatter(scale_inv * jnp.einsum('ax,soxp->asop', rows_part, grad_...]
    reduce_sum x0 -> x1, other arithmetic: none -> 12.3 us  [shards(): grad_spec = jnp.sum(lax.all_gather(local_spec, 'dp'), axis=0)]
    all_gather x1, blocking collectives: 7.42 us -> 17.6 us  [shards(): lax.all_gather(mixed_modes, 'gz', axis=0, tiled=True)]
    dot_general x2, matrix products: 24.5 us -> 17.3 us  [to_modes(): lax.dot_general(flattened, kron, contract_cells, precision=highest)]
  transfers between devices with their start and end apart: 3 -> 3, of which waited for: 3 -> 2; matrix products, arithmetic and copies ran while one was open for 14% -> 15% of each run, Pallas kernels for 0% -> 0%
where the time goes in v1:
time: 660 us; the launch traced here: 650 us
  blocking collectives  412 us (62%)
  matrix products  141 us (21%)
  waiting for transfers between devices  31.1 us (5%)
  local copies, waits for them, and re-layouts  28.4 us (4%)
  other arithmetic  23.4 us (4%)
  between operations  14.3 us (2%)
    psum x1, blocking collectives, shards(): total_point, total_bias = lax.psum((local_point, local_bias), ('dp', 'gz'))  387 us
    dot_general x2, matrix products, add_inverse(): return jnp.einsum('ax,asoz->soxz', row_basis, inner, precision=highest)  50.9 us
    reduce_scatter x1, waiting for transfers between devices, shards(): lax.psum_scatter(scale_inv * jnp.einsum('ax,soxp->asop', rows_part, grad_...  26.1 us
    mul x2, local copies, waits for them, and re-layouts, kron_table(): outer = basis[:, None, :, None] * basis[None, :, None, :]  25.8 us
    dot_general x2, matrix products, add_inverse(): jnp.dot(piece.reshape(piece_rows * samples_dev * channels, M * M), kron,...  24.2 us
    dot_general x1, matrix products, shards(): jnp.einsum('sixz,soxz->io', field, grad_pre, preferred_element_type=jnp.f...  19.9 us
    all_gather x1, blocking collectives, shards(): lax.all_gather(mixed_modes, 'gz', axis=0, tiled=True)  17.6 us
    dot_general x2, matrix products, to_modes(): lax.dot_general(flattened, kron, contract_cells, precision=highest)  17.3 us
  transfers between devices with their start and end apart: 3, of which 2 were waited for; matrix products, arithmetic and copies ran while one was open for 15% of the time, Pallas kernels for 0%

profile of v1, /device:TPU:0, one launch (start us, length us, event | category | flops | bytes accessed | tf_op | source)
XLA Modules:
  0.0 650.4 jit_solution(12257270693698853265)
XLA Ops:
  7.4 6.2 broadcast_multiply_fusion
  13.6 12.9 %mul.213 = f32[256,9216]{1,0:T(8,128)} reshape(f32[16,16,96,96]{3,2,1,0:T(8,128)} %broadcast_multiply_fusion) | data formatting | bytes 18874368 | tf_op jit(solution)/shard_map/mul | solution.py:24
  26.5 11.1 %convolution_bitcast_fusion = f32[384,256]{0,1:T(8,128)S(1)} fusion(f32[256,9216]{1,0:T(8,128)} %mul.213, bf16[384,9216]{1,0:T(8,128)(2,1)} %bitcast.100), kind=kOutput, calls=%fused_computation.20 | convolution fusion | flops 10871635968 | bytes 16908288 | tf_op jit(solution)/shard_map/dot_general | solution.py:47
  38.2 0.9 copy.32
  39.1 12.9 %reshape.212 = f32[256,9216,1]{1,0,2:T(8,128)} reshape(f32[16,16,96,96]{3,2,1,0:T(8,128)} %broadcast_multiply_fusion) | data formatting | bytes 18874368 | tf_op jit(solution)/shard_map/mul | solution.py:24
  52.0 11.7 %fusion.13 = f32[16,24,9216]{2,0,1:T(8,128)} fusion(bf16[16,24,9216]{2,1,0:T(8,128)(2,1)} %bitcast.101, bf16[16,16]{1,0:T(8,128)(2,1)S(1)} %copy-done), kind=kOutput, calls=%fused_computation.18 | convolution fusion | flops 113246208 | bytes 21234176 | tf_op jit(solution)/shard_map/sixz,io->soxz/dot_general | solution.py:71
  63.7 4.9 reduce-scatter.3.cloned.1.call-done
  68.7 1.0 multiply_reduce_fusion.1
  69.7 17.6 %all_gather.12 = f32[16,1,16,256]{3,2,1,0:T(8,128)S(1)} all-gather(f32[4,1,16,256]{3,2,1,0:T(8,128)S(1)} %bitcast.109), channel_id=1, replica_groups=mesh['dp'=32,'gz'=4] {'gz'}, dimensions={0}, use_global_device_ids=true | all-gather | bytes 327680 | tf_op jit(solution)/shard_map/all_gather | solution.py:68
  87.3 12.0 %fusion.24 = f32[16,16,9216]{2,0,1:T(8,128)S(1)} fusion(f32[256,9216,1]{1,0,2:T(8,128)} %reshape.212, f32[16,1,16,256]{3,2,1,0:T(8,128)S(1)} %all_gather.12), kind=kOutput, calls=%fused_computation.32 | convolution fusion | flops 7247757312 | bytes 19136512 | tf_op jit(solution)/shard_map/dot_general | solution.py:53
  99.3 25.1 %convert_reduce_fusion = (f32[16]{0:T(128)S(1)}, bf16[1,16,24,9216]{3,2,1,0:T(8,128)(2,1)S(1)}) fusion(f32[16]{0:T(128)S(1)} %copy-done.4, f32[16,24,9216]{2,0,1:T(8,128)} %fusion.13, f32[16,16,9216]{2,0,1:T(8,128)S(1)} %fusion.24, f32[16,96]{1,0:T(8,128)S(1)} %sine_select_fusion, s32[]{:T(128)S(6)} %select_n.65, bf16[1,16,24,9216]{3,2,1,0:T(8,128)(2,1)} %param.6), kind=kOutput, calls=%fused_computation.11 | convolution fusion | flops 736100352 | bytes 37755012 | tf_op jit(solution)/shard_map/ax,asoz->soxz/dot_general | solution.py:57
  124.5 6.2 fusion.47
  131.1 0.9 copy.37
  132.4 26.1 %reduce-scatter.5.cloned.1.call-done = f32[4,1,16,256]{3,2,1,0:T(8,128)} async-done(((f32[16,1,16,256]{3,2,1,0:T(8,128)}), f32[4,1,16,256]{3,2,1,0:T(8,128)}) %reduce-scatter.5.cloned.1.call-update) | async-done | bytes 65552 | tf_op jit(solution)/shard_map/reduce_scatter | solution.py:77
  158.5 2.1 multiply_bitcast_fusion
  160.6 19.9 %fusion.17 = f32[16,16]{0,1:T(8,128)S(1)} fusion(bf16[16,24,9216]{2,1,0:T(8,128)(2,1)} %bitcast.102, bf16[16,24,9216]{2,1,0:T(8,128)(2,1)} %bitcast.103), kind=kOutput, calls=%fused_computation.25 | convolution fusion | flops 113246208 | bytes 14156800 | tf_op jit(solution)/shard_map/sixz,soxz->io/dot_general | solution.py:89
  180.5 387.2 %all-reduce = (f32[16,16]{0,1:T(8,128)S(1)}, f32[16]{0:T(128)S(1)}) all-reduce(f32[16,16]{0,1:T(8,128)S(1)} %fusion.17, f32[16]{0:T(128)S(1)} %get-tuple-element.20), channel_id=1, replica_groups=mesh['dp'=32,'gz'=4] {'dp','gz'}, use_global_device_ids=true, to_apply=%region_3.4 | all-reduce | flops 272 | bytes 2176 | tf_op jit(solution)/shard_map/psum | solution.py:91
  567.6 0.7 copy.43
  568.8 16.0 %fusion.10 = f32[24,9216,16]{1,2,0:T(8,128)} fusion(bf16[16,24,9216]{2,1,0:T(8,128)(2,1)} %bitcast.104, bf16[16,16]{1,0:T(8,128)(2,1)S(1)} %copy-done), kind=kOutput, calls=%fused_computation.15 | convolution fusion | flops 113246208 | bytes 21234176 | tf_op jit(solution)/shard_map/soxz,io->sixz/dot_general | solution.py:87
  584.8 7.3 %all_gather.13 = f32[16,1,16,256]{3,2,1,0:T(8,128)S(1)} all-gather(f32[4,1,16,256]{3,2,1,0:T(8,128)S(1)} %bitcast.108), channel_id=1, replica_groups=mesh['dp'=32,'gz'=4] {'gz'}, dimensions={0}, use_global_device_ids=true | all-gather | bytes 327680 | tf_op jit(solution)/shard_map/all_gather | solution.py:84
  592.1 12.2 %fusion.22 = f32[16,16,9216]{2,0,1:T(8,128)S(1)} fusion(f32[256,9216,1]{1,0,2:T(8,128)} %reshape.212, f32[16,1,16,256]{3,2,1,0:T(8,128)S(1)} %all_gather.13), kind=kOutput, calls=%fused_computation.30 | convolution fusion | flops 7247757312 | bytes 19136512 | tf_op jit(solution)/shard_map/dot_general | solution.py:53
  604.3 25.8 %fusion.6 = bf16[1,16,24,9216]{3,2,1,0:T(8,128)(2,1)} fusion(f32[24,9216,16]{1,2,0:T(8,128)} %fusion.10, f32[16,16,9216]{2,0,1:T(8,128)S(1)} %fusion.22, f32[16,96]{1,0:T(8,128)S(1)} %sine_select_fusion, s32[]{:T(128)S(6)} %select_n.65), kind=kOutput, calls=%fused_computation.8 | convolution fusion | flops 690094080 | bytes 30676996 | tf_op jit(solution)/shard_map/ax,asoz->soxz/dot_general | solution.py:57
  630.1 12.3 %reduce_sum.18 = f32[4,16,16,256]{3,2,1,0:T(8,128)S(1)} reduce(f32[32,4,16,16,256]{4,3,2,1,0:T(8,128)} %bitcast.99, f32[]{:T(128)} %constant.50.clone.1), dimensions={0}, to_apply=%region_2.3 | reduce | flops 8126464 | bytes 34603012 | tf_op jit(solution)/shard_map/reduce_sum | solution.py:93
  642.4 1.1 broadcast_multiply_fusion.1
  (32 shorter events, 2.3 us)
Async XLA Ops:
  7.2 44.9 %copy-start = (bf16[16,16]{1,0:T(8,128)(2,1)S(1)}, bf16[16,16]{1,0:T(8,128)(2,1)}, u32[]{:S(2)}) copy-start(bf16[16,16]{1,0:T(8,128)(2,1)} %param.8) | copy-start | bytes 1540
  7.2 61.5 %reduce-scatter.3.cloned.1.call-start = ((), (), s32[]{:S(2)}) async-start(), calls=%async_computation.2 | async-start | bytes 327680 | tf_op jit(solution)/shard_map/reduce_scatter | solution.py:61
  39.1 119.5 %reduce-scatter.5.cloned.1.call-start = ((), (), s32[]{:S(2)}) async-start(), calls=%async_computation.3 | async-start | bytes 327680 | tf_op jit(solution)/shard_map/reduce_scatter | solution.py:77
  52.0 16.7 %copy-start.2 = (f32[4,16,16,256]{3,2,1,0:T(8,128)S(1)}, f32[4,16,16,256]{3,2,1,0:T(8,128)}, u32[]{:S(2)}) copy-start(f32[4,16,16,256]{3,2,1,0:T(8,128)} %param.7) | copy-start | bytes 3145732
  87.3 12.0 %copy-start.4 = (f32[16]{0:T(128)S(1)}, f32[16]{0:T(128)}, u32[]{:S(2)}) copy-start(f32[16]{0:T(128)} %param.9) | copy-start | bytes 196
  87.3 37.2 %slice-start = ((s8[9437184]{0:T(1024)(128)(4,1)}), s8[4194304]{0:T(1024)(128)(4,1)S(1)}, s32[]{:S(2)}) async-start(s8[9437184]{0:T(1024)(128)(4,1)} %bitcast.97), calls=%async_computation.5 | async-start | bytes 8388608
  99.3 25.2 %slice-start.1 = ((s8[9437184]{0:T(1024)(128)(4,1)}), s8[4194304]{0:T(1024)(128)(4,1)S(1)}, s32[]{:S(2)}) async-start(s8[9437184]{0:T(1024)(128)(4,1)} %bitcast.97), calls=%async_computation.6 | async-start | bytes 8388608
  99.3 25.2 %slice-start.2 = ((s8[9437184]{0:T(1024)(128)(4,1)}), s8[1048576]{0:T(1024)(128)(4,1)S(1)}, s32[]{:S(2)}) async-start(s8[9437184]{0:T(1024)(128)(4,1)} %bitcast.97), calls=%async_computation.7 | async-start | bytes 2097152
  124.4 6.2 copy-start.1
  124.4 34.1 %copy-start.3 = (f32[4,1,16,256]{3,2,1,0:T(8,128)S(1)}, f32[4,1,16,256]{3,2,1,0:T(8,128)}, u32[]{:S(2)}) copy-start(f32[4,1,16,256]{3,2,1,0:T(8,128)} %reduce-scatter.3.cloned.1.call-done) | copy-start | bytes 196612
  132.0 498.1 %all-gather.3.cloned.1.call-start = ((), (), s32[]{:S(2)}) async-start(), calls=%async_computation.4 | async-start | bytes 34603008 | tf_op jit(solution)/shard_map/all_gather | solution.py:93
Sparse Core Ops, SparseCore 0:
  39.2 29.4 reduce-scatter.2
  132.1 26.3 reduce-scatter.4
  160.7 365.1 all-gather.2
